TPU v7x, 256 devices: a whole 4x4x8 slice. The times are simulated.
256 devices in a mesh: row: 32 (over z, y), col: 8 (over x, core).
Axes of the slice: x: 4, y: 4, z: 8, core: 2. Of those that a mesh axis runs over, the one named last changes fastest.
Arguments:
- factor: float32 [32, 3, 1024, 4, 1024], P('row', None, None, None, 'col'), may hold values from -0.01953125 to 0.01953125
- knowns: float32 [32, 3, 1024, 256], P('row'), may hold values from -6 to 6
- inverse: float32 [4, 1024, 1024], P(None, None, 'col'), may hold values from -0.1875 to 0.1875
Outputs:
- solved: float32 [4, 1024, 256], P(None, 'col', 'row')
All inputs are finite; a program needn't handle non-finite values.
Results may differ from a plain program's by a relative error of at most 0.0001.
Values sent between devices are 32-bit elements; how exact they have to be, the bound alone decides.
A program may use at most 64 MiB of HBM per device.

v0:
```python
import jax
import jax.numpy as jnp
from jax import lax
from jax.sharding import PartitionSpec as P

NBLK = 96
KW = 4


def from_root(value, axis, root):
    mine = lax.axis_index(axis) == root
    return lax.psum(jnp.where(mine, value, jnp.zeros_like(value)), axis)


def apply_inverse(residual, inverse_block):
    full_resid = lax.all_gather(residual, "col", axis=0, tiled=True)
    return jnp.einsum(
        "cm,cs->ms",
        inverse_block,
        full_resid,
        precision=lax.Precision.HIGHEST,
        preferred_element_type=jnp.float32,
    )


def spread_block(own_factor, local_slot, solved_part):
    rows_block = own_factor[local_slot]
    return jnp.einsum(
        "ajc,as->jcs",
        rows_block,
        lax.all_gather(solved_part, "col", axis=0, tiled=True),
        precision=lax.Precision.HIGHEST,
        preferred_element_type=jnp.float32,
    )


def own_sources(stacked, row_index, row_count):
    source_width = stacked.shape[2] // row_count
    return lax.dynamic_slice_in_dim(stacked, row_index * source_width, source_width, 2)


def on_device(factor, knowns, inverse):
    row_count = lax.axis_size("row")
    row_index = lax.axis_index("row")
    col_index = lax.axis_index("col")
    slice_width = factor.shape[4]
    first_block = NBLK - KW
    own_factor = factor[0]
    own_knowns = knowns[0]
    counted = lax.iota(jnp.int32, own_knowns.shape[0]) * row_count + row_index
    keep_mask = (counted < first_block).astype(jnp.float32)
    prefix = jnp.einsum(
        "lajc,las->jcs",
        own_factor,
        own_knowns * keep_mask[:, None, None],
        precision=lax.Precision.HIGHEST,
        preferred_element_type=jnp.float32,
    )
    owned_rhs = []
    for step in range(KW):
        block_id = first_block + step
        rhs_slice = lax.dynamic_slice_in_dim(
            own_knowns[block_id // row_count], col_index * slice_width, slice_width, 0
        )
        owner_mask = (row_index == block_id % row_count).astype(jnp.float32)
        owned_rhs.append(owner_mask * rhs_slice)
    local_terms = prefix - jnp.stack(owned_rhs)
    correction = jnp.zeros_like(local_terms)
    solved_parts = []
    totals = lax.psum(local_terms, "row")
    for step in range(KW):
        block_id = first_block + step
        residual = -(totals[step] + correction[step])
        solved_part = apply_inverse(residual, inverse[step])
        solved_parts.append(solved_part)
        if step + 1 < KW:
            contrib = spread_block(own_factor, block_id // row_count, solved_part)
            correction = correction + from_root(contrib, "row", block_id % row_count)
    return own_sources(jnp.stack(solved_parts), row_index, row_count)


def solution(mesh):
    return jax.shard_map(
        on_device,
        mesh=mesh,
        in_specs=(
            P("row", None, None, None, "col"),
            P("row", None, None, None),
            P(None, None, "col"),
        ),
        out_specs=P(None, "col", "row"),
        check_vma=False,
    )
```

profile of v0, /device:TPU:1, one launch (start us, length us, event | category | flops | bytes accessed | tf_op | source)
XLA Modules:
  0.0 832.3 jit_solution(10658403784603572605)
XLA Ops:
  6.6 1.2 slice-done
  7.8 0.1 copy.12
  7.9 10.2 %fusion.18 = f32[4,128,256]{1,2,0:T(8,128)} fusion(f32[3,1024,4,128]{3,2,1,0:T(4,128)} %bitcast.101, f32[1,3,1024,256]{3,2,1,0:T(8,128)} %param.4, f32[3]{0:T(128)S(1)} %compare_convert_fusion, f32[1,128,256]{1,2,0:T(8,128)S(1)} %get-tuple-element.6, f32[1,128,256]{1,2,0:T(8,128)S(1)} %get-tuple-element.7, f32[1,128,256]{1,2,0:T(8,128)S(1)} %get-tuple-element.8, ...), kind=kOutput, calls=%fused_computation.16 | convolution fusion | flops 4833148928 | bytes 10485772 | tf_op jit(solution)/shard_map/lajc,las->jcs/dot_general | solution.py:52
  18.1 0.0 all-reduce.5.cloned.1.call-update
  18.1 0.0 all-gather.18.cloned.1.call-start
  18.2 148.2 %all-reduce.5.cloned.1.call-done = f32[4,128,256]{1,2,0:T(8,128)} async-done(((f32[4,128,256]{1,2,0:T(8,128)}), f32[4,128,256]{1,2,0:T(8,128)}) %all-reduce.5.cloned.1.call-update) | async-done | bytes 524304 | tf_op jit(solution)/shard_map/psum | solution.py:70
  166.4 1.6 slice_negate_fusion
  168.0 0.0 all-gather.18.cloned.1.call-update
  168.0 0.0 all-gather.12.cloned.1.call-start
  168.0 27.9 %all-gather.18.cloned.1.call-done = f32[1,1024,256]{1,2,0:T(8,128)} async-done(((f32[1,128,256]{1,2,0:T(8,128)}), f32[1,1024,256]{1,2,0:T(8,128)}) %all-gather.18.cloned.1.call-update) | async-done | bytes 1048592 | tf_op jit(solution)/shard_map/all_gather | solution.py:16
  195.9 3.0 fusion.31
  198.9 0.0 all-gather.12.cloned.1.call-update
  199.0 0.0 all-reduce.7.cloned.1.call-start
  199.0 1.7 slice.50
  200.8 25.2 %all-gather.12.cloned.1.call-done = f32[1024,256]{0,1:T(8,128)} async-done(((f32[128,256]{0,1:T(8,128)}), f32[1024,256]{0,1:T(8,128)}) %all-gather.12.cloned.1.call-update) | async-done | bytes 1048592 | tf_op jit(solution)/shard_map/all_gather | solution.py:31
  225.9 4.0 fusion.13
  229.9 0.0 all-reduce.7.cloned.1.call-update
  229.9 0.0 all-gather.20.cloned.1.call-start
  230.0 145.1 %all-reduce.7.cloned.1.call-done = f32[4,128,256]{1,2,0:T(8,128)} async-done(((f32[4,128,256]{1,2,0:T(8,128)}), f32[4,128,256]{1,2,0:T(8,128)}) %all-reduce.7.cloned.1.call-update) | async-done | bytes 524304 | tf_op jit(solution)/shard_map/psum | solution.py:12
  375.0 1.6 fusion.44
  376.6 0.0 all-gather.20.cloned.1.call-update
  376.7 0.0 all-gather.14.cloned.1.call-start
  376.7 27.8 %all-gather.20.cloned.1.call-done = f32[1,1024,256]{1,2,0:T(8,128)} async-done(((f32[1,128,256]{1,2,0:T(8,128)}), f32[1,1024,256]{1,2,0:T(8,128)}) %all-gather.20.cloned.1.call-update) | async-done | bytes 1048592 | tf_op jit(solution)/shard_map/all_gather | solution.py:16
  404.5 3.0 fusion.28
  407.5 0.0 all-gather.14.cloned.1.call-update
  407.5 0.2 all-reduce.9.cloned.1.call-start
  407.8 26.7 %all-gather.14.cloned.1.call-done = f32[1024,256]{0,1:T(8,128)} async-done(((f32[128,256]{0,1:T(8,128)}), f32[1024,256]{0,1:T(8,128)}) %all-gather.14.cloned.1.call-update) | async-done | bytes 1048592 | tf_op jit(solution)/shard_map/all_gather | solution.py:31
  434.5 4.0 fusion.15
  438.5 0.0 all-gather.22.cloned.1.call-start
  438.5 145.1 %all-reduce.9.cloned.1.call-done = f32[4,128,256]{1,2,0:T(8,128)} async-done(((f32[4,128,256]{1,2,0:T(8,128)}), f32[4,128,256]{1,2,0:T(8,128)}) %all-reduce.9.cloned.1.call-update) | async-done | bytes 524304 | tf_op jit(solution)/shard_map/psum | solution.py:12
  583.6 1.1 add.49
  584.7 1.6 fusion.43
  586.3 0.0 all-gather.22.cloned.1.call-update
  586.3 0.0 all-gather.16.cloned.1.call-start
  586.4 27.8 %all-gather.22.cloned.1.call-done = f32[1,1024,256]{1,2,0:T(8,128)} async-done(((f32[1,128,256]{1,2,0:T(8,128)}), f32[1,1024,256]{1,2,0:T(8,128)}) %all-gather.22.cloned.1.call-update) | async-done | bytes 1048592 | tf_op jit(solution)/shard_map/all_gather | solution.py:16
  614.2 3.0 fusion.25
  617.2 0.0 all-gather.16.cloned.1.call-update
  617.2 0.0 all-reduce.11.cloned.1.call-start
  617.2 26.9 %all-gather.16.cloned.1.call-done = f32[1024,256]{0,1:T(8,128)} async-done(((f32[128,256]{0,1:T(8,128)}), f32[1024,256]{0,1:T(8,128)}) %all-gather.16.cloned.1.call-update) | async-done | bytes 1048592 | tf_op jit(solution)/shard_map/all_gather | solution.py:31
  644.1 4.0 fusion.17
  648.1 0.0 all-reduce.11.cloned.1.call-update
  648.1 0.0 all-gather.24.cloned.1.call-start
  648.1 145.1 %all-reduce.11.cloned.1.call-done = f32[4,128,256]{1,2,0:T(8,128)} async-done(((f32[4,128,256]{1,2,0:T(8,128)}), f32[4,128,256]{1,2,0:T(8,128)}) %all-reduce.11.cloned.1.call-update) | async-done | bytes 524304 | tf_op jit(solution)/shard_map/psum | solution.py:12
  793.2 1.6 fusion.42
  794.8 0.0 all-gather.24.cloned.1.call-update
  794.9 27.9 %all-gather.24.cloned.1.call-done = f32[1,1024,256]{1,2,0:T(8,128)} async-done(((f32[1,128,256]{1,2,0:T(8,128)}), f32[1,1024,256]{1,2,0:T(8,128)}) %all-gather.24.cloned.1.call-update) | async-done | bytes 1048592 | tf_op jit(solution)/shard_map/all_gather | solution.py:16
  822.7 2.3 convolution_bitcast_fusion
  825.1 0.6 fusion.47
  (14 shorter events, 0.1 us)
Async XLA Ops:
  6.5 1.2 slice-start
  6.5 159.9 %all-reduce.5.cloned.1.call-start = ((), (), s32[]{:S(2)}) async-start(), calls=%async_computation | async-start | bytes 1048576 | tf_op jit(solution)/shard_map/psum | solution.py:70
  18.1 177.8 %all-gather.18.cloned.1.call-start = ((), (), s32[]{:S(2)}) async-start(), calls=%async_computation.7 | async-start | bytes 1179648 | tf_op jit(solution)/shard_map/all_gather | solution.py:16
  168.0 57.9 %all-gather.12.cloned.1.call-start = ((), (), s32[]{:S(2)}) async-start(), calls=%async_computation.1 | async-start | bytes 1179648 | tf_op jit(solution)/shard_map/all_gather | solution.py:31
  199.0 176.0 %all-reduce.7.cloned.1.call-start = ((), (), s32[]{:S(2)}) async-start(), calls=%async_computation.2 | async-start | bytes 1048576 | tf_op jit(solution)/shard_map/psum | solution.py:12
  229.9 174.6 %all-gather.20.cloned.1.call-start = ((), (), s32[]{:S(2)}) async-start(), calls=%async_computation.8 | async-start | bytes 1179648 | tf_op jit(solution)/shard_map/all_gather | solution.py:16
  376.7 57.8 %all-gather.14.cloned.1.call-start = ((), (), s32[]{:S(2)}) async-start(), calls=%async_computation.3 | async-start | bytes 1179648 | tf_op jit(solution)/shard_map/all_gather | solution.py:31
  407.5 176.1 %copy-start.3 = (f32[4,128,256]{1,2,0:T(8,128)S(1)}, f32[4,128,256]{1,2,0:T(8,128)}, u32[]{:S(2)}) copy-start(f32[4,128,256]{1,2,0:T(8,128)} %all-reduce.7.cloned.1.call-done) | copy-start | bytes 1572868
  407.5 176.1 %all-reduce.9.cloned.1.call-start = ((), (), s32[]{:S(2)}) async-start(), calls=%async_computation.4 | async-start | bytes 1048576 | tf_op jit(solution)/shard_map/psum | solution.py:12
  438.5 175.7 %all-gather.22.cloned.1.call-start = ((), (), s32[]{:S(2)}) async-start(), calls=%async_computation.9 | async-start | bytes 1179648 | tf_op jit(solution)/shard_map/all_gather | solution.py:16
  586.3 57.8 %all-gather.16.cloned.1.call-start = ((), (), s32[]{:S(2)}) async-start(), calls=%async_computation.5 | async-start | bytes 1179648 | tf_op jit(solution)/shard_map/all_gather | solution.py:31
  617.2 176.0 %all-reduce.11.cloned.1.call-start = ((), (), s32[]{:S(2)}) async-start(), calls=%async_computation.6 | async-start | bytes 1048576 | tf_op jit(solution)/shard_map/psum | solution.py:12
  648.1 177.0 %copy-start = (f32[256,128]{1,0:T(8,128)S(1)}, f32[256,128]{1,0:T(8,128)}, u32[]{:S(2)}) copy-start(f32[256,128]{1,0:T(8,128)} %fusion.31) | copy-start | bytes 393220
  648.1 177.1 %copy-start.1 = (f32[256,128]{1,0:T(8,128)S(1)}, f32[256,128]{1,0:T(8,128)}, u32[]{:S(2)}) copy-start(f32[256,128]{1,0:T(8,128)} %fusion.28) | copy-start | bytes 393220
  648.1 177.1 %copy-start.2 = (f32[256,128]{1,0:T(8,128)S(1)}, f32[256,128]{1,0:T(8,128)}, u32[]{:S(2)}) copy-start(f32[256,128]{1,0:T(8,128)} %fusion.25) | copy-start | bytes 393220
  648.1 174.7 %all-gather.24.cloned.1.call-start = ((), (), s32[]{:S(2)}) async-start(), calls=%async_computation.10 | async-start | bytes 1179648 | tf_op jit(solution)/shard_map/all_gather | solution.py:16
Sparse Core Ops, SparseCore 0:
  18.2 148.1 all-reduce.4
  168.2 27.6 all-gather.17
  199.1 26.7 all-gather.11
  230.0 144.9 all-reduce.6
  376.8 27.6 all-gather.19
  407.7 26.7 all-gather.13
  438.6 144.9 all-reduce.8
  586.4 27.6 all-gather.21
  617.3 26.7 all-gather.15
  648.2 144.9 all-reduce.10
  795.0 27.6 all-gather.23
where the time goes:
time: 833 us; the launch traced here: 832 us
  waiting for transfers between devices  774 us (93%)
  matrix products  33.4 us (4%)
  between operations  13.3 us (2%)
    psum x3, waiting for transfers between devices, from_root(): return lax.psum(jnp.where(mine, value, jnp.zeros_like(value)), axis)  435 us
    psum x1, waiting for transfers between devices, on_device(): totals = lax.psum(local_terms, 'row')  148 us
    all_gather x4, waiting for transfers between devices, apply_inverse(): full_resid = lax.all_gather(residual, 'col', axis=0, tiled=True)  111 us
    all_gather x3, waiting for transfers between devices, spread_block(): lax.all_gather(solved_part, 'col', axis=0, tiled=True)  78.7 us
  transfers between devices with their start and end apart: 11, of which 11 were waited for; matrix products, arithmetic and copies ran while one was open for 0% of the time, Pallas kernels for 0%

commit v1 on v0

v1 whole, which is shorter than its diff:
```python
import jax
import jax.numpy as jnp
from jax import lax
from jax.experimental import pallas as pl
from jax.experimental.pallas import tpu as pltpu
from jax.sharding import PartitionSpec as P

MESH = pl.DeviceIdType.MESH
KW = 4
NY = 4
LANE = 128
STEP = 512
PARTS = 4
F32 = jnp.float32
BF16 = jnp.bfloat16
POINTS = (3, 5, 8, 12)
HOP = 2


def halves(value):
    high = value.astype(BF16)
    low = (value - high.astype(F32)).astype(BF16)
    return high, low


def mul(a, b):
    return jnp.dot(a, b, preferred_element_type=F32)


def kernel(
    sizes,
    fac, kn, inv, out,
    fbuf, kbuf, dbuf, kth, ktl, acc, ybuf, zsrc, zbuf, tfull, racc, cbuf, lhs,
    dh, dl, ubuf, uh, ul, xfull, csrc, obuf,
    fsem, ksem, dsem, ysend, yrecv, zsend, zrecv, tsend, trecv, xsend, xrecv,
    csend, crecv, usend, urecv, osend, orecv,
):
    nz, nc, nl, nb, ns = sizes
    sp = ns // nz
    so = sp // NY
    per = nb // STEP
    row, col = lax.axis_index("row"), lax.axis_index("col")
    z, y = lax.div(row, NY), lax.rem(row, NY)
    last = nz - 1
    nblk = NY - 1 - y
    nf = nblk * PARTS
    ends = (NY - 1) * PARTS + HOP * (nz - 1)
    crows = nb // (2 * PARTS)

    def remote(src, dst, ssem, rsem, to_row, to_col):
        return pltpu.make_async_remote_copy(
            src_ref=src, dst_ref=dst, send_sem=ssem, recv_sem=rsem,
            device_id=(to_row, to_col), device_id_type=MESH,
        )

    def load_f(c):
        rows = pl.ds(c * STEP * KW, STEP * KW)
        return pltpu.make_async_copy(fac.at[rows], fbuf.at[rows], fsem.at[c])

    def load_k(c):
        rows = pl.ds(c * STEP, STEP)
        return pltpu.make_async_copy(kn.at[rows], kbuf.at[rows], ksem.at[c])

    def load_d():
        return pltpu.make_async_copy(inv.at[y], dbuf, dsem)

    steps = nl * per
    own = (nl - 1) * per

    @pl.when(z == last)
    def _():
        for c in range(own, steps):
            load_f(c).start()

    for c in range(own):
        load_f(c).start()
        load_k(c).start()

    @pl.when(z < last)
    def _():
        for c in range(own, steps):
            load_f(c).start()

    for c in range(own, steps):
        load_k(c).start()
    load_d().start()

    barrier = pltpu.get_barrier_semaphore()
    for dy in range(NY):
        for dk in range(nc):
            if dy or dk:
                pl.semaphore_signal(
                    barrier, inc=1,
                    device_id=(z * NY + lax.rem(y + dy, NY), lax.rem(col + dk, nc)),
                    device_id_type=MESH,
                )
    for d in range(1, nz):
        pl.semaphore_signal(
            barrier, inc=1, device_id=(lax.rem(z + d, nz) * NY + y, col), device_id_type=MESH
        )
    pl.semaphore_wait(barrier, NY * nc - 1 + nz - 1)

    def piece(way, f):
        first = way * (nb // 2) + lax.rem(f, PARTS) * crows
        return ubuf.at[lax.div(f, PARTS), pl.ds(pl.multiple_of(first, 8), crows)]

    def pass_on(way, f):
        to = lax.rem(z + (1 if way == 0 else nz - 1), nz)
        part = piece(way, f)
        return remote(part, part, usend.at[way, f], urecv.at[way, f], to * NY + y, col)

    @pl.when(z == last)
    def _():
        for c in range(own, steps):
            load_f(c).wait()

        @pl.loop(0, nf)
        def _(f):
            j = y + 1 + lax.div(f, PARTS)
            for way in (0, 1):
                first = way * (nb // 2) + lax.rem(f, PARTS) * crows
                start = (nl - 1) * nb * KW + first * KW + j
                ubuf[lax.div(f, PARTS), pl.ds(pl.multiple_of(first, 8), crows), :] = fbuf[
                    pl.ds(start, crows, stride=KW), :
                ]
                pass_on(way, f).start()

    def at_end(way):
        return (z == last - 1) if way == 0 else (z == 0)

    def relay(since, until):
        @pl.when(z < last)
        def _():
            @pl.loop(since, until)
            def _(t):
                for way in (0, 1):
                    hop = z + 1 if way == 0 else last - z
                    f = t - HOP * hop

                    @pl.when(jnp.logical_and(f >= 0, f < nf))
                    def _():
                        pass_on(way, f).wait_recv()

                        @pl.when(jnp.logical_not(at_end(way)))
                        def _():
                            pass_on(way, f).start()

    def multiply(c, half, first):
        rows = pl.ds(pl.multiple_of(c * STEP, STEP), STEP)
        if half == 0:
            load_f(c).wait()
            load_k(c).wait()
            high, low = halves(kbuf[rows, :].T)
            kth[c] = high
            ktl[c] = low
        else:
            high, low = kth[c], ktl[c]
        fh, fl = [], []
        for j in (2 * half, 2 * half + 1):
            a, b = halves(fbuf[pl.ds(c * STEP * KW + j, STEP, stride=KW), :])
            fh.append(a)
            fl.append(b)
        fh, fl = jnp.concatenate(fh, axis=1), jnp.concatenate(fl, axis=1)
        got = mul(high, fh) + mul(low, fh) + mul(high, fl)
        for n in (0, 1):
            part = got[:, n * LANE:(n + 1) * LANE]
            if first:
                acc[2 * half + n] = part
            else:
                acc[2 * half + n] += part

    def to_row(j):
        slot = lax.rem(y - j + NY, NY) - 1
        return remote(acc.at[j], ybuf.at[slot], ysend.at[j], yrecv.at[slot], z * NY + j, col)

    for half in (0, 1):
        multiply(0, half, True)

        @pl.loop(1, own)
        def _(c):
            multiply(c, half, False)

        @pl.when(z < last)
        def _():
            @pl.loop(own, steps)
            def _(c):
                multiply(c, half, False)

        for j in (2 * half, 2 * half + 1):
            @pl.when(y != j)
            def _():
                to_row(j).start()

        relay(0 if half == 0 else POINTS[half - 1], POINTS[half])

    load_d().wait()
    for c in range(per):
        rows = pl.ds(c * STEP, STEP)
        a, b = halves(dbuf[rows, :])
        dh[rows, :] = a
        dl[rows, :] = b

    @pl.when(z == last)
    def _():
        for c in range(own, steps):
            load_k(c).wait()
        first = pl.multiple_of((nl - 1) * nb + col * LANE, LANE)
        acc[y] -= kbuf[pl.ds(first, LANE), :].T

    for slot in range(NY - 1):
        remote(acc.at[0], ybuf.at[slot], ysend.at[0], yrecv.at[slot], row, col).wait_recv()
    zsrc[...] = acc[y] + ybuf[0] + ybuf[1] + ybuf[2]

    def to_plane(d):
        to = lax.rem(z + d, nz)
        return remote(
            zsrc.at[pl.ds(pl.multiple_of(to * sp, 8), sp)], zbuf.at[d - 1],
            zsend.at[d - 1], zrecv.at[d - 1], to * NY + y, col,
        )

    for d in range(1, nz):
        to_plane(d).start()
    relay(POINTS[1], POINTS[2])
    total = zsrc[pl.ds(pl.multiple_of(z * sp, 8), sp), :]
    for d in range(1, nz):
        to_plane(d).wait_recv()
        total += zbuf[d - 1]
    tfull[col] = total

    def to_cols(full, ssem, rsem, d):
        return remote(full.at[col], full.at[col], ssem.at[d - 1], rsem.at[d - 1], row, lax.rem(col + d, nc))

    def from_cols(full, ssem, rsem, d):
        slot = lax.rem(col - d + nc, nc)
        return remote(full.at[slot], full.at[slot], ssem.at[d - 1], rsem.at[d - 1], row, col)

    for d in range(1, nc):
        to_cols(tfull, tsend, trecv, d).start()
    relay(POINTS[2], POINTS[3])
    for d in range(1, nc):
        from_cols(tfull, tsend, trecv, d).wait_recv()
    racc[...] = -tfull[...]

    def split_u():
        @pl.loop(0, nblk)
        def _(b):
            for c in range(per):
                rows = pl.ds(c * STEP, STEP)
                a, l = halves(ubuf[b, rows, :])
                uh[b, rows, :] = a
                ul[b, rows, :] = l

    @pl.when(y > 0)
    def _():
        relay(POINTS[3], ends)
        split_u()

    @pl.loop(0, y)
    def _(i):
        for k in range(nc):
            remote(csrc.at[0], cbuf.at[i, k], csend.at[0, k], crecv.at[i, k], row, col).wait_recv()
        racc[...] -= cbuf[i]

    def fill(full):
        for k in range(nc):
            a, b = halves(full[k])
            lhs[0:sp, k * LANE:(k + 1) * LANE] = a
            lhs[sp:2 * sp, k * LANE:(k + 1) * LANE] = b

    def apply(high, low):
        both = mul(lhs[...], high)
        return both[0:sp] + both[sp:2 * sp] + mul(lhs[0:sp, :], low)

    fill(racc)
    xfull[col] = apply(dh[...], dl[...])

    @pl.when(y < NY - 1)
    def _():
        for d in range(1, nc):
            to_cols(xfull, xsend, xrecv, d).start()

    def to_owner(d):
        to = lax.rem(y + d, NY)
        return remote(
            xfull.at[col, pl.ds(pl.multiple_of(to * so, 8), so)], obuf.at[y],
            osend.at[d - 1], orecv.at[d - 1], z * NY + to, col,
        )

    for d in range(1, NY):
        to_owner(d).start()
    obuf[y] = xfull[col, pl.ds(pl.multiple_of(y * so, 8), so), :]

    @pl.when(y == 0)
    def _():
        relay(POINTS[3], ends)
        split_u()

    def to_later(b, k):
        return remote(
            csrc.at[b], cbuf.at[y, col], csend.at[b, k], crecv.at[y, col], z * NY + y + 1 + b, k
        )

    @pl.when(y < NY - 1)
    def _():
        for d in range(1, nc):
            from_cols(xfull, xsend, xrecv, d).wait_recv()
        fill(xfull)

        @pl.loop(0, nblk)
        def _(b):
            csrc[b] = apply(uh[b], ul[b])
            for k in range(nc):
                to_later(b, k).start()

    for d in range(1, NY):
        slot = lax.rem(y - d + NY, NY)
        remote(obuf.at[slot], obuf.at[slot], osend.at[d - 1], orecv.at[d - 1], row, col).wait_recv()
    out[...] = obuf[...]

    for j in range(NY):
        @pl.when(y != j)
        def _():
            to_row(j).wait_send()
    for d in range(1, nz):
        to_plane(d).wait_send()
    for d in range(1, nc):
        to_cols(tfull, tsend, trecv, d).wait_send()

    @pl.when(y < NY - 1)
    def _():
        for d in range(1, nc):
            to_cols(xfull, xsend, xrecv, d).wait_send()

        @pl.loop(0, nblk)
        def _(b):
            for k in range(nc):
                to_later(b, k).wait_send()

    for d in range(1, NY):
        to_owner(d).wait_send()

    @pl.loop(0, nf)
    def _(f):
        for way in (0, 1):
            @pl.when(jnp.logical_not(at_end(way)))
            def _():
                pass_on(way, f).wait_send()


def on_device(nz, nc, factor, knowns, inverse):
    _, nl, nb, _, lanes = factor.shape
    ns = knowns.shape[3]
    sp = ns // nz
    steps = nl * (nb // STEP)
    V, DMA = pltpu.VMEM, pltpu.SemaphoreType.DMA
    scratch = [
        V((nl * nb * KW, LANE), F32), V((nl * nb, ns), F32), V((nb, LANE), F32),
        V((steps, ns, STEP), BF16), V((steps, ns, STEP), BF16),
        V((KW, ns, LANE), F32), V((NY - 1, ns, LANE), F32),
        V((ns, LANE), F32), V((nz - 1, sp, LANE), F32),
        V((nc, sp, LANE), F32), V((nc, sp, LANE), F32),
        V((NY - 1, nc, sp, LANE), F32), V((2 * sp, nb), BF16),
        V((nb, LANE), BF16), V((nb, LANE), BF16),
        V((NY - 1, nb, LANE), F32), V((NY - 1, nb, LANE), BF16), V((NY - 1, nb, LANE), BF16),
        V((nc, sp, LANE), F32), V((NY - 1, sp, LANE), F32), V((KW, sp // NY, LANE), F32),
        DMA((steps,)), DMA((steps,)), DMA(()), DMA((NY,)), DMA((NY - 1,)),
        DMA((nz - 1,)), DMA((nz - 1,)), DMA((nc - 1,)), DMA((nc - 1,)), DMA((nc - 1,)), DMA((nc - 1,)),
        DMA((NY - 1, nc)), DMA((NY - 1, nc)),
        DMA((2, (NY - 1) * PARTS)), DMA((2, (NY - 1) * PARTS)), DMA((NY - 1,)), DMA((NY - 1,)),
    ]
    hbm = pl.BlockSpec(memory_space=pl.ANY)

    def body(*refs):
        kernel((nz, nc, nl, nb, ns), *refs)

    got = pl.pallas_call(
        body,
        out_shape=jax.ShapeDtypeStruct((KW, sp // NY, LANE), F32),
        in_specs=[hbm, hbm, hbm],
        out_specs=pl.BlockSpec(memory_space=pltpu.VMEM),
        scratch_shapes=scratch,
        compiler_params=pltpu.CompilerParams(
            collective_id=0, has_side_effects=True, vmem_limit_bytes=56 * 2 ** 20
        ),
        name="solve_window",
    )(
        factor.reshape(nl * nb * KW, lanes),
        knowns.reshape(nl * nb, ns),
        inverse,
    )
    return jnp.transpose(got, (0, 2, 1))


def solution(mesh):
    nz, nc = mesh.shape["row"] // NY, mesh.shape["col"]

    def step(factor, knowns, inverse):
        return on_device(nz, nc, factor, knowns, inverse)

    return jax.shard_map(
        step,
        mesh=mesh,
        in_specs=(
            P("row", None, None, None, "col"),
            P("row", None, None, None),
            P(None, None, "col"),
        ),
        out_specs=P(None, "col", "row"),
        check_vma=False,
    )
```

time: 833 us -> 93.6 us (0.11)
  waiting for transfers between devices: 774 us -> 0 us
  Pallas kernels: 0 us -> 92.1 us
  matrix products: 33.4 us -> 0 us
  between operations: 13.3 us -> 0.01 us
    psum x4 -> x0, waiting for transfers between devices: 583 us -> none  [the longest x3 435 us: from_root(): return lax.psum(jnp.where(mine, value, jnp.zeros_like(value)), axis)]
    all_gather x7 -> x0, waiting for transfers between devices: 190 us -> none  [the longest x4 111 us: apply_inverse(): full_resid = lax.all_gather(residual, 'col', axis=0, tiled=True)]
    pallas_call x0 -> x1, Pallas kernels: none -> 92.1 us  [on_device(): pl.pallas_call(body, out_shape=jax.ShapeDtypeStruct((KW, sp // NY, LANE),...]
    dot_general x8 -> x0, matrix products: 33.4 us -> none  [the longest x3 11.9 us: spread_block(): jnp.einsum('ajc,as->jcs', rows_block, lax.all_gather(solved_part, 'col',...]
  transfers between devices with their start and end apart: 11 -> 0, of which waited for: 11 -> 0; matrix products, arithmetic and copies ran while one was open for 0% -> 0% of each run, Pallas kernels for 0% -> 0%
where the time goes in v1:
time: 93.6 us; the launch traced here: 93.4 us
  Pallas kernels  92.1 us (98%)
  local copies, waits for them, and re-layouts  1.32 us (1%)
    pallas_call x1, Pallas kernels, on_device(): pl.pallas_call(body, out_shape=jax.ShapeDtypeStruct((KW, sp // NY, LANE),...  92.1 us

profile of v1, /device:TPU:1, one launch (start us, length us, event | category | flops | bytes accessed | tf_op | source)
XLA Modules:
  0.0 93.4 jit_solution(4254462626062449326)
XLA Ops:
  0.0 92.1 %solve_window.1 = f32[4,8,128]{2,1,0:T(8,128)} custom-call(f32[12288,128]{1,0:T(8,128)} %bitcast.3, f32[3072,256]{1,0:T(8,128)} %bitcast.4, f32[4,1024,128]{2,1,0:T(8,128)} %refs_2_.1), custom_call_target="tpu_custom_call" | custom-call | tf_op jit(solution)/shard_map/solve_window/pallas_call | solution.py:376
  92.1 1.3 %copy.5 = f32[4,128,8]{1,2,0:T(8,128)} copy(f32[4,128,8]{1,2,0:T(8,128)} %bitcast.5) | data formatting | bytes 32768

commit v2 on v1

--- a/solution.py
+++ b/solution.py
@@ -10,11 +10,12 @@
 NY = 4
 LANE = 128
 STEP = 512
-PARTS = 4
+TILE = 256
+PARTS = 8
 F32 = jnp.float32
 BF16 = jnp.bfloat16
-POINTS = (3, 5, 8, 12)
-HOP = 2
+POINTS = (2, 10, 22, 30)
+HOP = 4
 
 
 def halves(value):
@@ -30,10 +31,10 @@
 def kernel(
     sizes,
     fac, kn, inv, out,
-    fbuf, kbuf, dbuf, kth, ktl, acc, ybuf, zsrc, zbuf, tfull, racc, cbuf, lhs,
-    dh, dl, ubuf, uh, ul, xfull, csrc, obuf,
+    fbuf, kbuf, dfull, kth, ktl, acc, ybuf, zsrc, zbuf, tfull, racc, cbuf, lhs,
+    dh, dl, ubuf, uh, ul, wh, wl, xfull, csrc, obuf,
     fsem, ksem, dsem, ysend, yrecv, zsend, zrecv, tsend, trecv, xsend, xrecv,
-    csend, crecv, usend, urecv, osend, orecv,
+    csend, crecv, usend, urecv, osend, orecv, dsend, drecv,
 ):
     nz, nc, nl, nb, ns = sizes
     sp = ns // nz
@@ -44,7 +45,6 @@
     last = nz - 1
     nblk = NY - 1 - y
     nf = nblk * PARTS
-    ends = (NY - 1) * PARTS + HOP * (nz - 1)
     crows = nb // (2 * PARTS)
 
     def remote(src, dst, ssem, rsem, to_row, to_col):
@@ -62,10 +62,12 @@
         return pltpu.make_async_copy(kn.at[rows], kbuf.at[rows], ksem.at[c])
 
     def load_d():
-        return pltpu.make_async_copy(inv.at[y], dbuf, dsem)
+        return pltpu.make_async_copy(inv.at[y], dfull.at[col], dsem)
 
     steps = nl * per
     own = (nl - 1) * per
+
+    load_d().start()
 
     @pl.when(z == last)
     def _():
@@ -83,7 +85,6 @@
 
     for c in range(own, steps):
         load_k(c).start()
-    load_d().start()
 
     barrier = pltpu.get_barrier_semaphore()
     for dy in range(NY):
@@ -98,7 +99,6 @@
         pl.semaphore_signal(
             barrier, inc=1, device_id=(lax.rem(z + d, nz) * NY + y, col), device_id_type=MESH
         )
-    pl.semaphore_wait(barrier, NY * nc - 1 + nz - 1)
 
     def piece(way, f):
         first = way * (nb // 2) + lax.rem(f, PARTS) * crows
@@ -109,21 +109,68 @@
         part = piece(way, f)
         return remote(part, part, usend.at[way, f], urecv.at[way, f], to * NY + y, col)
 
-    @pl.when(z == last)
-    def _():
-        for c in range(own, steps):
-            load_f(c).wait()
-
-        @pl.loop(0, nf)
-        def _(f):
-            j = y + 1 + lax.div(f, PARTS)
-            for way in (0, 1):
-                first = way * (nb // 2) + lax.rem(f, PARTS) * crows
-                start = (nl - 1) * nb * KW + first * KW + j
-                ubuf[lax.div(f, PARTS), pl.ds(pl.multiple_of(first, 8), crows), :] = fbuf[
-                    pl.ds(start, crows, stride=KW), :
-                ]
-                pass_on(way, f).start()
+    def feed():
+        @pl.when(z == last)
+        def _():
+            for c in range(own, steps):
+                load_f(c).wait()
+
+            @pl.loop(0, nf)
+            def _(f):
+                j = y + 1 + lax.div(f, PARTS)
+                for way in (0, 1):
+                    first = way * (nb // 2) + lax.rem(f, PARTS) * crows
+                    start = (nl - 1) * nb * KW + first * KW + j
+                    ubuf[lax.div(f, PARTS), pl.ds(pl.multiple_of(first, 8), crows), :] = fbuf[
+                        pl.ds(start, crows, stride=KW), :
+                    ]
+                    pass_on(way, f).start()
+
+    core = lax.rem(col, 2)
+    partner = col + 1 - 2 * core
+    middle = jnp.logical_and(y > 0, y < NY - 1)
+
+    def d_slot(d):
+        return lax.rem(col + 2 * d, nc)
+
+    def d_out(d):
+        mine = dfull.at[col]
+        return remote(mine, mine, dsend.at[d], drecv.at[col], row, d_slot(d) if d else partner)
+
+    def d_relay(d):
+        part = dfull.at[d_slot(d)]
+        return remote(part, part, dsend.at[nc // 2 - 1 + d], drecv.at[d_slot(d)], row, partner)
+
+    def d_in(slot):
+        part = dfull.at[slot]
+        return remote(part, part, dsend.at[0], drecv.at[slot], row, partner)
+
+    def share_d():
+        load_d().wait()
+
+        @pl.when(middle)
+        def _():
+            for d in range(nc // 2):
+                d_out(d).start()
+
+    def take_d():
+        for d in range(1, nc // 2):
+            d_in(d_slot(d)).wait_recv()
+            d_relay(d).start()
+        for d in range(nc // 2):
+            d_in(lax.rem(partner + 2 * d, nc)).wait_recv()
+
+    def fold(count):
+        high = jnp.concatenate([uh[b] for b in range(count)], axis=1)
+        low = jnp.concatenate([ul[b] for b in range(count)], axis=1)
+
+        @pl.loop(0, nb // TILE)
+        def _(c):
+            rows = pl.ds(pl.multiple_of(c * TILE, TILE), TILE)
+            a, l = halves(jnp.concatenate([dfull[k, rows, :] for k in range(nc)], axis=1))
+            got = mul(a, high) + mul(l, high) + mul(a, low)
+            for b in range(count):
+                wh[b, rows, :], wl[b, rows, :] = halves(got[:, b * LANE:(b + 1) * LANE])
 
     def at_end(way):
         return (z == last - 1) if way == 0 else (z == 0)
@@ -175,6 +222,10 @@
 
     for half in (0, 1):
         multiply(0, half, True)
+        if half == 0:
+            pl.semaphore_wait(barrier, NY * nc - 1 + nz - 1)
+            feed()
+            share_d()
 
         @pl.loop(1, own)
         def _(c):
@@ -193,10 +244,9 @@
 
         relay(0 if half == 0 else POINTS[half - 1], POINTS[half])
 
-    load_d().wait()
     for c in range(per):
         rows = pl.ds(c * STEP, STEP)
-        a, b = halves(dbuf[rows, :])
+        a, b = halves(dfull[col, rows, :])
         dh[rows, :] = a
         dl[rows, :] = b
 
@@ -239,21 +289,30 @@
     relay(POINTS[2], POINTS[3])
     for d in range(1, nc):
         from_cols(tfull, tsend, trecv, d).wait_recv()
-    racc[...] = -tfull[...]
-
-    def split_u():
-        @pl.loop(0, nblk)
-        def _(b):
-            for c in range(per):
-                rows = pl.ds(c * STEP, STEP)
-                a, l = halves(ubuf[b, rows, :])
-                uh[b, rows, :] = a
-                ul[b, rows, :] = l
-
-    @pl.when(y > 0)
-    def _():
-        relay(POINTS[3], ends)
-        split_u()
+    racc[...] = tfull[...]
+
+    def split_u(b):
+        for c in range(per):
+            rows = pl.ds(c * STEP, STEP)
+            a, l = halves(ubuf[b, rows, :])
+            uh[b, rows, :] = a
+            ul[b, rows, :] = l
+
+    def finish(b):
+        so_far = POINTS[3] if b == 0 else max(POINTS[3], PARTS * b + HOP * (nz - 1))
+        relay(so_far, PARTS * (b + 1) + HOP * (nz - 1))
+        split_u(b)
+
+    for b in range(NY - 2):
+        @pl.when(jnp.logical_and(y > 0, b < nblk))
+        def _():
+            finish(b)
+
+    for count in range(1, NY - 1):
+        @pl.when(y == NY - 1 - count)
+        def _():
+            take_d()
+            fold(count)
 
     @pl.loop(0, y)
     def _(i):
@@ -271,10 +330,26 @@
         both = mul(lhs[...], high)
         return both[0:sp] + both[sp:2 * sp] + mul(lhs[0:sp, :], low)
 
+    def to_later(b, k):
+        return remote(
+            csrc.at[b], cbuf.at[y, col], csend.at[b, k], crecv.at[y, col], z * NY + y + 1 + b, k
+        )
+
+    def correct(b, high, low):
+        csrc[b] = apply(high[b], low[b])
+        for k in range(nc):
+            to_later(b, k).start()
+
     fill(racc)
+    for count in range(1, NY - 1):
+        @pl.when(y == NY - 1 - count)
+        def _():
+            for b in range(count):
+                correct(b, wh, wl)
+
     xfull[col] = apply(dh[...], dl[...])
 
-    @pl.when(y < NY - 1)
+    @pl.when(y == 0)
     def _():
         for d in range(1, nc):
             to_cols(xfull, xsend, xrecv, d).start()
@@ -292,25 +367,14 @@
 
     @pl.when(y == 0)
     def _():
-        relay(POINTS[3], ends)
-        split_u()
-
-    def to_later(b, k):
-        return remote(
-            csrc.at[b], cbuf.at[y, col], csend.at[b, k], crecv.at[y, col], z * NY + y + 1 + b, k
-        )
-
-    @pl.when(y < NY - 1)
-    def _():
+        finish(0)
         for d in range(1, nc):
             from_cols(xfull, xsend, xrecv, d).wait_recv()
         fill(xfull)
-
-        @pl.loop(0, nblk)
-        def _(b):
-            csrc[b] = apply(uh[b], ul[b])
-            for k in range(nc):
-                to_later(b, k).start()
+        for b in range(NY - 1):
+            if b > 0:
+                finish(b)
+            correct(b, uh, ul)
 
     for d in range(1, NY):
         slot = lax.rem(y - d + NY, NY)
@@ -326,15 +390,22 @@
     for d in range(1, nc):
         to_cols(tfull, tsend, trecv, d).wait_send()
 
-    @pl.when(y < NY - 1)
+    @pl.when(y == 0)
     def _():
         for d in range(1, nc):
             to_cols(xfull, xsend, xrecv, d).wait_send()
 
-        @pl.loop(0, nblk)
-        def _(b):
-            for k in range(nc):
-                to_later(b, k).wait_send()
+    @pl.loop(0, nblk)
+    def _(b):
+        for k in range(nc):
+            to_later(b, k).wait_send()
+
+    @pl.when(middle)
+    def _():
+        for d in range(nc // 2):
+            d_out(d).wait_send()
+        for d in range(1, nc // 2):
+            d_relay(d).wait_send()
 
     for d in range(1, NY):
         to_owner(d).wait_send()
@@ -354,7 +425,7 @@
     steps = nl * (nb // STEP)
     V, DMA = pltpu.VMEM, pltpu.SemaphoreType.DMA
     scratch = [
-        V((nl * nb * KW, LANE), F32), V((nl * nb, ns), F32), V((nb, LANE), F32),
+        V((nl * nb * KW, LANE), F32), V((nl * nb, ns), F32), V((nc, nb, LANE), F32),
         V((steps, ns, STEP), BF16), V((steps, ns, STEP), BF16),
         V((KW, ns, LANE), F32), V((NY - 1, ns, LANE), F32),
         V((ns, LANE), F32), V((nz - 1, sp, LANE), F32),
@@ -362,11 +433,13 @@
         V((NY - 1, nc, sp, LANE), F32), V((2 * sp, nb), BF16),
         V((nb, LANE), BF16), V((nb, LANE), BF16),
         V((NY - 1, nb, LANE), F32), V((NY - 1, nb, LANE), BF16), V((NY - 1, nb, LANE), BF16),
+        V((NY - 2, nb, LANE), BF16), V((NY - 2, nb, LANE), BF16),
         V((nc, sp, LANE), F32), V((NY - 1, sp, LANE), F32), V((KW, sp // NY, LANE), F32),
         DMA((steps,)), DMA((steps,)), DMA(()), DMA((NY,)), DMA((NY - 1,)),
         DMA((nz - 1,)), DMA((nz - 1,)), DMA((nc - 1,)), DMA((nc - 1,)), DMA((nc - 1,)), DMA((nc - 1,)),
         DMA((NY - 1, nc)), DMA((NY - 1, nc)),
         DMA((2, (NY - 1) * PARTS)), DMA((2, (NY - 1) * PARTS)), DMA((NY - 1,)), DMA((NY - 1,)),
+        DMA((nc - 1,)), DMA((nc,)),
     ]
     hbm = pl.BlockSpec(memory_space=pl.ANY)
 
@@ -388,7 +461,7 @@
         knowns.reshape(nl * nb, ns),
         inverse,
     )
-    return jnp.transpose(got, (0, 2, 1))
+    return -jnp.transpose(got, (0, 2, 1))
 
 
 def solution(mesh):

time: 93.6 us -> 70.8 us (0.76)
  Pallas kernels: 92.1 us -> 69.3 us
  other arithmetic: 0 us -> 1.33 us
  local copies, waits for them, and re-layouts: 1.32 us -> 0 us
    pallas_call x1, Pallas kernels: 92.1 us -> 69.3 us  [on_device(): pl.pallas_call(body, out_shape=jax.ShapeDtypeStruct((KW, sp // NY, LANE),...]
    neg x0 -> x1, other arithmetic: none -> 1.33 us  [on_device(): return -jnp.transpose(got, (0, 2, 1))]
    unnamed x1 -> x0, local copies, waits for them, and re-layouts: 1.32 us -> none
where the time goes in v2:
time: 70.8 us; the launch traced here: 70.7 us
  Pallas kernels  69.3 us (98%)
  other arithmetic  1.33 us (2%)
    pallas_call x1, Pallas kernels, on_device(): pl.pallas_call(body, out_shape=jax.ShapeDtypeStruct((KW, sp // NY, LANE),...  69.3 us

profile of v2, /device:TPU:1, one launch (start us, length us, event | category | flops | bytes accessed | tf_op | source)
XLA Modules:
  0.0 70.7 jit_solution(8418321786412253233)
XLA Ops:
  0.0 69.3 %solve_window.1 = f32[4,8,128]{2,1,0:T(8,128)} custom-call(f32[12288,128]{1,0:T(8,128)} %bitcast.4, f32[3072,256]{1,0:T(8,128)} %bitcast.5, f32[4,1024,128]{2,1,0:T(8,128)} %refs_2_.1), custom_call_target="tpu_custom_call" | custom-call | tf_op jit(solution)/shard_map/solve_window/pallas_call | solution.py:449
  69.3 1.3 %negate_bitcast_fusion = f32[4,128,8]{1,2,0:T(8,128)} fusion(f32[4,8,128]{2,1,0:T(8,128)} %solve_window.1), kind=kLoop, calls=%fused_computation | loop fusion | flops 4096 | bytes 32768 | tf_op jit(solution)/shard_map/neg | solution.py:464

commit v3 on v2

--- a/solution.py
+++ b/solution.py
@@ -14,7 +14,7 @@
 PARTS = 8
 F32 = jnp.float32
 BF16 = jnp.bfloat16
-POINTS = (2, 10, 22, 30)
+POINTS = (6, 15, 26, 33)
 HOP = 4
 
 
@@ -100,6 +100,9 @@
             barrier, inc=1, device_id=(lax.rem(z + d, nz) * NY + y, col), device_id_type=MESH
         )
 
+    def enter():
+        pl.semaphore_wait(barrier, NY * nc - 1 + nz - 1)
+
     def piece(way, f):
         first = way * (nb // 2) + lax.rem(f, PARTS) * crows
         return ubuf.at[lax.div(f, PARTS), pl.ds(pl.multiple_of(first, 8), crows)]
@@ -110,21 +113,19 @@
         return remote(part, part, usend.at[way, f], urecv.at[way, f], to * NY + y, col)
 
     def feed():
-        @pl.when(z == last)
-        def _():
-            for c in range(own, steps):
-                load_f(c).wait()
-
-            @pl.loop(0, nf)
-            def _(f):
-                j = y + 1 + lax.div(f, PARTS)
-                for way in (0, 1):
-                    first = way * (nb // 2) + lax.rem(f, PARTS) * crows
-                    start = (nl - 1) * nb * KW + first * KW + j
-                    ubuf[lax.div(f, PARTS), pl.ds(pl.multiple_of(first, 8), crows), :] = fbuf[
-                        pl.ds(start, crows, stride=KW), :
-                    ]
-                    pass_on(way, f).start()
+        for c in range(own, steps):
+            load_f(c).wait()
+
+        @pl.loop(0, nf)
+        def _(f):
+            j = y + 1 + lax.div(f, PARTS)
+            for way in (0, 1):
+                first = way * (nb // 2) + lax.rem(f, PARTS) * crows
+                start = (nl - 1) * nb * KW + first * KW + j
+                ubuf[lax.div(f, PARTS), pl.ds(pl.multiple_of(first, 8), crows), :] = fbuf[
+                    pl.ds(start, crows, stride=KW), :
+                ]
+                pass_on(way, f).start()
 
     core = lax.rem(col, 2)
     partner = col + 1 - 2 * core
@@ -161,16 +162,14 @@
             d_in(lax.rem(partner + 2 * d, nc)).wait_recv()
 
     def fold(count):
-        high = jnp.concatenate([uh[b] for b in range(count)], axis=1)
-        low = jnp.concatenate([ul[b] for b in range(count)], axis=1)
+        high, low = uh[count], ul[count]
 
         @pl.loop(0, nb // TILE)
         def _(c):
             rows = pl.ds(pl.multiple_of(c * TILE, TILE), TILE)
             a, l = halves(jnp.concatenate([dfull[k, rows, :] for k in range(nc)], axis=1))
             got = mul(a, high) + mul(l, high) + mul(a, low)
-            for b in range(count):
-                wh[b, rows, :], wl[b, rows, :] = halves(got[:, b * LANE:(b + 1) * LANE])
+            wh[count, rows, :], wl[count, rows, :] = halves(got)
 
     def at_end(way):
         return (z == last - 1) if way == 0 else (z == 0)
@@ -221,28 +220,40 @@
         return remote(acc.at[j], ybuf.at[slot], ysend.at[j], yrecv.at[slot], z * NY + j, col)
 
     for half in (0, 1):
+        if half == 0:
+            @pl.when(z == last)
+            def _():
+                enter()
+                feed()
+
         multiply(0, half, True)
         if half == 0:
-            pl.semaphore_wait(barrier, NY * nc - 1 + nz - 1)
-            feed()
+            @pl.when(z < last)
+            def _():
+                enter()
+
             share_d()
 
         @pl.loop(1, own)
         def _(c):
             multiply(c, half, False)
+            if half == 1:
+                relay(POINTS[0] + c - 1, POINTS[0] + c)
 
         @pl.when(z < last)
         def _():
             @pl.loop(own, steps)
             def _(c):
                 multiply(c, half, False)
+                if half == 1:
+                    relay(POINTS[0] + c - 1, POINTS[0] + c)
 
         for j in (2 * half, 2 * half + 1):
             @pl.when(y != j)
             def _():
                 to_row(j).start()
 
-        relay(0 if half == 0 else POINTS[half - 1], POINTS[half])
+        relay(0 if half == 0 else POINTS[0] + steps - 1, POINTS[half])
 
     for c in range(per):
         rows = pl.ds(c * STEP, STEP)
@@ -303,16 +314,16 @@
         relay(so_far, PARTS * (b + 1) + HOP * (nz - 1))
         split_u(b)
 
-    for b in range(NY - 2):
+    @pl.when(middle)
+    def _():
+        finish(0)
+        take_d()
+        fold(0)
+
+    for b in range(1, NY - 2):
         @pl.when(jnp.logical_and(y > 0, b < nblk))
         def _():
             finish(b)
-
-    for count in range(1, NY - 1):
-        @pl.when(y == NY - 1 - count)
-        def _():
-            take_d()
-            fold(count)
 
     @pl.loop(0, y)
     def _(i):
@@ -345,6 +356,8 @@
         @pl.when(y == NY - 1 - count)
         def _():
             for b in range(count):
+                if b:
+                    fold(b)
                 correct(b, wh, wl)
 
     xfull[col] = apply(dh[...], dl[...])

time: 70.8 us -> 67.6 us (0.955)
  Pallas kernels: 69.3 us -> 66.1 us
    pallas_call x1, Pallas kernels: 69.3 us -> 66.1 us  [on_device(): pl.pallas_call(body, out_shape=jax.ShapeDtypeStruct((KW, sp // NY, LANE),...]
where the time goes in v3:
time: 67.6 us; the launch traced here: 67.4 us
  Pallas kernels  66.1 us (98%)
  other arithmetic  1.33 us (2%)
    pallas_call x1, Pallas kernels, on_device(): pl.pallas_call(body, out_shape=jax.ShapeDtypeStruct((KW, sp // NY, LANE),...  66.1 us

profile of v3, /device:TPU:1, one launch (start us, length us, event | category | flops | bytes accessed | tf_op | source)
XLA Modules:
  0.0 67.4 jit_solution(8578276242142171723)
XLA Ops:
  0.0 66.1 %solve_window.1 = f32[4,8,128]{2,1,0:T(8,128)} custom-call(f32[12288,128]{1,0:T(8,128)} %bitcast.4, f32[3072,256]{1,0:T(8,128)} %bitcast.5, f32[4,1024,128]{2,1,0:T(8,128)} %refs_2_.1), custom_call_target="tpu_custom_call" | custom-call | tf_op jit(solution)/shard_map/solve_window/pallas_call | solution.py:462
  66.1 1.3 %negate_bitcast_fusion = f32[4,128,8]{1,2,0:T(8,128)} fusion(f32[4,8,128]{2,1,0:T(8,128)} %solve_window.1), kind=kLoop, calls=%fused_computation | loop fusion | flops 4096 | bytes 32768 | tf_op jit(solution)/shard_map/neg | solution.py:477

commit v4 on v3

--- a/solution.py
+++ b/solution.py
@@ -67,24 +67,10 @@
     steps = nl * per
     own = (nl - 1) * per
 
-    load_d().start()
-
     @pl.when(z == last)
     def _():
         for c in range(own, steps):
             load_f(c).start()
-
-    for c in range(own):
-        load_f(c).start()
-        load_k(c).start()
-
-    @pl.when(z < last)
-    def _():
-        for c in range(own, steps):
-            load_f(c).start()
-
-    for c in range(own, steps):
-        load_k(c).start()
 
     barrier = pltpu.get_barrier_semaphore()
     for dy in range(NY):
@@ -99,6 +85,20 @@
         pl.semaphore_signal(
             barrier, inc=1, device_id=(lax.rem(z + d, nz) * NY + y, col), device_id_type=MESH
         )
+
+    load_d().start()
+
+    for c in range(own):
+        load_f(c).start()
+        load_k(c).start()
+
+    @pl.when(z < last)
+    def _():
+        for c in range(own, steps):
+            load_f(c).start()
+
+    for c in range(own, steps):
+        load_k(c).start()
 
     def enter():
         pl.semaphore_wait(barrier, NY * nc - 1 + nz - 1)

time: 67.6 us -> 67.5 us (level)
  no operation moved by 1% of the time
where the time goes in v4:
time: 67.5 us; the launch traced here: 67.4 us
  Pallas kernels  66 us (98%)
  other arithmetic  1.33 us (2%)
    pallas_call x1, Pallas kernels, on_device(): pl.pallas_call(body, out_shape=jax.ShapeDtypeStruct((KW, sp // NY, LANE),...  66 us

profile of v4, /device:TPU:1, one launch (start us, length us, event | category | flops | bytes accessed | tf_op | source)
XLA Modules:
  0.0 67.4 jit_solution(717114727224668895)
XLA Ops:
  0.0 66.0 %solve_window.1 = f32[4,8,128]{2,1,0:T(8,128)} custom-call(f32[12288,128]{1,0:T(8,128)} %bitcast.4, f32[3072,256]{1,0:T(8,128)} %bitcast.5, f32[4,1024,128]{2,1,0:T(8,128)} %refs_2_.1), custom_call_target="tpu_custom_call" | custom-call | tf_op jit(solution)/shard_map/solve_window/pallas_call | solution.py:462
  66.0 1.3 %negate_bitcast_fusion = f32[4,128,8]{1,2,0:T(8,128)} fusion(f32[4,8,128]{2,1,0:T(8,128)} %solve_window.1), kind=kLoop, calls=%fused_computation | loop fusion | flops 4096 | bytes 32768 | tf_op jit(solution)/shard_map/neg | solution.py:477
